TPU v7x, 32 devices: a whole 2x2x4 slice. The times are simulated.
32 devices in a mesh: layer: 4 (over x, core), dp: 8 (over z, y).
Axes of the slice: x: 2, y: 2, z: 4, core: 2. Of those that a mesh axis runs over, the one named last changes fastest.
Arguments:
- out_grads: bfloat16 [4, 128, 16384], P('layer', None, 'dp'), may hold values from -3 to 3
- in_acts: bfloat16 [4, 128, 4096], P('layer', None, 'dp'), may hold values from -3 to 3
- out_basis: bfloat16 [4, 16384, 16384], P('layer', None, 'dp'), may hold values from -0.046875 to 0.046875
- in_basis: bfloat16 [4, 4096, 4096], P('layer', None, 'dp'), may hold values from -0.09375 to 0.09375
- eigenvalues: bfloat16 [4, 16384, 4096], P('layer', 'dp'), may hold values from 0.5 to 50
- out_store: bfloat16 [4, 16, 32, 16384], P('layer', 'dp'), may hold values from -0.046875 to 0.046875
- in_store: bfloat16 [4, 16, 32, 4096], P('layer', 'dp'), may hold values from -0.09375 to 0.09375
- counts: int32 [16], P('dp'), may hold values from 1 to 4096
- winners: int32 [4, 6], replicated, may hold values from 0 to 15
Outputs:
- influence: float32 [4, 6, 32], replicated
All inputs are finite; a program needn't handle non-finite values.
Results may differ from a plain program's by a relative error of at most 0.0055.
Values may be sent and summed in bfloat16 or wider, within the bound.
A program may use at most 192 MiB of HBM per device.

v0:
```python
import jax
import jax.numpy as jnp
from jax import lax
from jax.sharding import PartitionSpec as P

NQ = 4
TQ = 32
WIN = 6
R = 32
SPAN = 128
damping = 0.1


def on_device(
    out_grads, in_acts, out_basis, in_basis, eigenvalues, out_store, in_store, counts, winners
):
    out_local = out_basis[0]
    in_local = in_basis[0]
    out_width = out_local.shape[1]
    rows = out_local
    turned_out = jnp.dot(
        lax.all_gather(out_grads[0], "dp", axis=1, tiled=True),
        rows,
        preferred_element_type=jnp.float32,
    ).astype(jnp.bfloat16)
    rows = in_local
    turned_part = jnp.dot(
        lax.all_gather(in_acts[0], "dp", axis=1, tiled=True),
        rows,
        preferred_element_type=jnp.float32,
    ).astype(jnp.bfloat16)
    turned_in = lax.all_gather(turned_part, "dp", axis=1, tiled=True)
    left = turned_out.reshape(NQ, TQ, out_width)
    right = turned_in.reshape(NQ, TQ, turned_in.shape[1])
    product = jnp.einsum("qtf,qtd->qfd", left, right, preferred_element_type=jnp.float32)
    divisor = eigenvalues[0].astype(jnp.float32) + damping
    precond = (product / divisor[None]).astype(jnp.bfloat16)
    alive = (jnp.arange(R, dtype=jnp.int32)[None, :] * SPAN < counts[:, None]).astype(jnp.bfloat16)
    masked = in_store[0] * alive[:, :, None]
    out_slices = lax.all_to_all(out_store[0], "dp", split_axis=2, concat_axis=0, tiled=True)
    chosen = winners.reshape(NQ * WIN)
    left_rows = jnp.take(out_slices, chosen, axis=0).reshape(NQ, WIN * R, out_width)
    full_width = turned_in.shape[1]
    in_whole = lax.all_gather(masked, "dp", axis=0, tiled=True)
    right_rows = jnp.take(in_whole, chosen, axis=0).reshape(NQ, WIN * R, full_width)
    mapped = jnp.einsum("qfd,qkd->qkf", precond, right_rows, preferred_element_type=jnp.float32)
    partial_value = jnp.sum(mapped * left_rows.astype(jnp.float32), axis=2)
    totals = lax.psum(partial_value, ("layer", "dp"))
    return totals.reshape(NQ, WIN, R)


def solution(mesh):
    placed = (
        P("layer", None, "dp"),
        P("layer", None, "dp"),
        P("layer", None, "dp"),
        P("layer", None, "dp"),
        P("layer", "dp", None),
        P("layer", "dp", None, None),
        P("layer", "dp", None, None),
        P("dp"),
        P(),
    )
    return jax.shard_map(on_device, mesh=mesh, in_specs=placed, out_specs=P(), check_vma=False)
```

profile of v0, /device:TPU:0, one launch (start us, length us, event | category | flops | bytes accessed | tf_op | source)
XLA Modules:
  0.0 364.3 jit_solution(16281501123913025915)
XLA Ops:
  6.5 0.0 all-gather.13.cloned.1.call-start
  6.5 0.7 all-gather.13.cloned.1.call-update
  7.3 0.0 all-gather.11.cloned.1.call-start
  7.3 0.7 all-gather.11.cloned.1.call-update
  8.0 0.0 all-gather.7.cloned.1.call-start
  8.1 0.7 compare_convert_fusion
  8.8 2.0 bitcast_multiply_fusion
  10.7 0.0 all-gather.7.cloned.1.call-update
  10.8 17.2 %copy.13 = bf16[1,2,32,16384]{2,1,3,0:T(2,128)(2,1)} copy(bf16[1,2,32,16384]{3,2,1,0:T(8,128)(2,1)} %param.14) | data formatting | bytes 4194304 | tf_op args[5]
  28.0 8.0 %bitcast_bitcast_fusion = bf16[16384,2,32]{2,1,0:T(2,128)(2,1)} fusion(bf16[1,2,32,16384]{2,1,3,0:T(2,128)(2,1)} %copy.13), kind=kLoop, calls=%fused_computation.25 | loop fusion | bytes 4194304
  36.0 0.0 copy-start.1
  36.0 11.2 %reshape.112 = bf16[8,2,65536]{2,1,0:T(2,128)(2,1)} reshape(bf16[16384,2,32]{2,1,0:T(2,128)(2,1)} %bitcast_bitcast_fusion) | data formatting | bytes 4194304
  47.2 7.3 %all-to-all-start = ((bf16[8,2,65536]{2,1,0:T(2,128)(2,1)}), bf16[8,2,65536]{2,1,0:T(2,128)(2,1)S(1)}, u32[]{:S(2)}, u32[]{:S(2)}) async-start(bf16[8,2,65536]{2,1,0:T(2,128)(2,1)} %reshape.112), calls=%async_computation | async-start | bytes 4194304 | tf_op jit(solution)/shard_map/all_to_all | solution.py:40
  54.5 0.0 all-gather.9.cloned.1.call-start
  54.6 0.0 copy-done.1
  54.6 0.1 reshape.90
  54.7 0.1 broadcast_in_dim.28
  54.8 0.1 broadcast_in_dim.29
  54.9 18.8 %add_bitcast_fusion = f32[2048,4096]{1,0:T(8,128)} fusion(bf16[1,2048,4096]{2,1,0:T(8,128)(2,1)} %param.13), kind=kLoop, calls=%fused_computation.6 | loop fusion | flops 16777216 | bytes 50331648 | tf_op jit(solution)/shard_map/div | solution.py:37
  73.7 0.0 all-gather.13.cloned.1.call-done
  73.7 3.9 %fusion.13 = bf16[128,512]{1,0:T(8,128)(2,1)} fusion(bf16[1,4096,512]{2,1,0:T(8,128)(2,1)} %param.12, bf16[1,128,4096]{2,1,0:T(8,128)(2,1)} %all-gather.13.cloned.1.call-done), kind=kOutput, calls=%fused_computation.15 | convolution fusion | flops 536936448 | bytes 5373952 | tf_op jit(solution)/shard_map/dot_general | solution.py:27
  77.6 0.0 all-gather.9.cloned.1.call-update
  77.6 50.9 %all-to-all-done = bf16[8,2,65536]{2,1,0:T(2,128)(2,1)S(1)} async-done(((bf16[8,2,65536]{2,1,0:T(2,128)(2,1)}), bf16[8,2,65536]{2,1,0:T(2,128)(2,1)S(1)}, u32[]{:S(2)}, u32[]{:S(2)}) %all-to-all-start) | async-done | bytes 2097184 | tf_op jit(solution)/shard_map/all_to_all | solution.py:40
  128.5 6.5 %reshape.113 = bf16[16384,2,32]{2,1,0:T(2,128)(2,1)} reshape(bf16[8,2,65536]{2,1,0:T(2,128)(2,1)S(1)} %all-to-all-done) | data formatting | bytes 4194304
  135.0 17.8 %copy.18 = bf16[2,32,8,2048]{3,1,0,2:T(8,128)(2,1)S(1)} copy(bf16[2,32,8,2048]{1,0,3,2:T(2,128)(2,1)} %bitcast.47) | data formatting | bytes 4194304 | tf_op jit(solution)/shard_map/all_to_all | solution.py:40
  152.8 2.5 gather_fusion.1
  155.3 0.0 all-gather.11.cloned.1.call-done
  155.3 26.3 %fusion.8 = bf16[128,2048]{1,0:T(8,128)(2,1)} fusion(bf16[1,16384,2048]{2,1,0:T(8,128)(2,1)} %param.11, bf16[1,128,16384]{2,1,0:T(8,128)(2,1)} %all-gather.11.cloned.1.call-done), kind=kOutput, calls=%fused_computation.14 | convolution fusion | flops 8590196736 | bytes 71827456 | tf_op jit(solution)/shard_map/dot_general | solution.py:21
  181.5 46.3 %all-gather.7.cloned.1.call-done = bf16[16,32,4096]{2,1,0:T(8,128)(2,1)} async-done(((bf16[2,32,4096]{2,1,0:T(8,128)(2,1)}), bf16[16,32,4096]{2,1,0:T(8,128)(2,1)}) %all-gather.7.cloned.1.call-update) | async-done | bytes 4194320 | tf_op jit(solution)/shard_map/all_gather | solution.py:44
  227.8 6.5 %gather_fusion = bf16[24,32,4096]{2,1,0:T(8,128)(2,1)} fusion(bf16[16,32,4096]{2,1,0:T(8,128)(2,1)} %all-gather.7.cloned.1.call-done, s32[1024]{0:T(1024)S(1)} %pad_clamp_fusion), kind=kCustom, calls=%fused_computation | custom fusion | bytes 12583008 | tf_op jit(solution)/shard_map/jit(_take)/gather | solution.py:45
  234.3 6.1 %bitcast_select_fusion = bf16[4,192,4096]{2,1,0:T(8,128)(2,1)} fusion(pred[4,192]{1,0:T(4,128)(4,1)S(1)} %broadcast_in_dim.29, bf16[4,192,4096]{2,1,0:T(8,128)(2,1)} %bitcast.48), kind=kLoop, calls=%fused_computation.8 | loop fusion | flops 3145728 | bytes 12583680 | tf_op jit(solution)/shard_map/jit(_take)/select_n | solution.py:45
  240.5 27.2 %all-gather.9.cloned.1.call-done = bf16[128,4096]{1,0:T(8,128)(2,1)} async-done(((bf16[128,512]{1,0:T(8,128)(2,1)}), bf16[128,4096]{1,0:T(8,128)(2,1)}) %all-gather.9.cloned.1.call-update) | async-done | bytes 1048592 | tf_op jit(solution)/shard_map/all_gather | solution.py:32
  267.7 0.0 copy-start
  267.7 45.8 %fusion.2 = f32[4,192,2048]{2,1,0:T(8,128)} fusion(bf16[4,192,4096]{2,1,0:T(8,128)(2,1)} %bitcast_select_fusion, f32[2048,4096]{1,0:T(8,128)} %add_bitcast_fusion, bf16[4,32,2048]{2,1,0:T(8,128)(2,1)} %bitcast.51, bf16[4,32,4096]{2,1,0:T(8,128)(2,1)} %bitcast.52), kind=kOutput, calls=%fused_computation.5 | convolution fusion | flops 15099494400 | bytes 47710208 | tf_op jit(solution)/shard_map/qfd,qkd->qkf/dot_general | solution.py:46
  313.5 0.0 copy-done
  313.5 3.8 %multiply_reduce_fusion = f32[4,192]{1,0:T(4,128)S(1)} fusion(f32[4,192,2048]{2,1,0:T(8,128)} %fusion.2, pred[4,192]{1,0:T(4,128)(4,1)S(1)} %broadcast_in_dim.29, bf16[4,192,2048]{2,1,0:T(8,128)(2,1)S(1)} %bitcast.50), kind=kLoop, calls=%fused_computation.9 | loop fusion | flops 6290688 | bytes 9441024 | tf_op jit(solution)/shard_map/reduce_sum | solution.py:47
  317.3 0.1 reshape.93
  317.4 39.8 %psum.7 = f32[4,6,32]{2,1,0:T(8,128)S(1)} all-reduce(f32[4,6,32]{2,1,0:T(8,128)S(1)} %reshape.93), channel_id=1, replica_groups=mesh['layer'=4,'dp'=8] {'layer','dp'}, use_global_device_ids=true, to_apply=%region_1.2 | all-reduce | flops 768 | bytes 6144 | tf_op jit(solution)/shard_map/psum | solution.py:48
  357.2 0.6 copy.16
  (4 shorter events, 0.0 us)
Async XLA Ops:
  6.5 67.1 %all-gather.13.cloned.1.call-start = ((), (), s32[]{:S(2)}) async-start(), calls=%async_computation.4 | async-start | bytes 1179648 | tf_op jit(solution)/shard_map/all_gather | solution.py:28
  7.3 148.0 %all-gather.11.cloned.1.call-start = ((), (), s32[]{:S(2)}) async-start(), calls=%async_computation.3 | async-start | bytes 4718592 | tf_op jit(solution)/shard_map/all_gather | solution.py:22
  8.0 219.8 %all-gather.7.cloned.1.call-start = ((), (), s32[]{:S(2)}) async-start(), calls=%async_computation.1 | async-start | bytes 4718592 | tf_op jit(solution)/shard_map/all_gather | solution.py:44
  36.0 18.6 %copy-start.1 = (s32[4,6]{1,0:T(4,128)S(1)}, s32[4,6]{1,0:T(4,128)}, u32[]{:S(2)}) copy-start(s32[4,6]{1,0:T(4,128)} %param.17) | copy-start | bytes 292
  47.2 81.3 %all-to-all-start = ((bf16[8,2,65536]{2,1,0:T(2,128)(2,1)}), bf16[8,2,65536]{2,1,0:T(2,128)(2,1)S(1)}, u32[]{:S(2)}, u32[]{:S(2)}) async-start(bf16[8,2,65536]{2,1,0:T(2,128)(2,1)} %reshape.112), calls=%async_computation | async-start | bytes 4194304 | tf_op jit(solution)/shard_map/all_to_all | solution.py:40
  54.5 213.1 %all-gather.9.cloned.1.call-start = ((), (), s32[]{:S(2)}) async-start(), calls=%async_computation.2 | async-start | bytes 1179648 | tf_op jit(solution)/shard_map/all_gather | solution.py:32
  267.7 45.8 %copy-start = (bf16[24,32,2048]{2,1,0:T(8,128)(2,1)S(1)}, bf16[24,32,2048]{2,1,0:T(8,128)(2,1)}, u32[]{:S(2)}) copy-start(bf16[24,32,2048]{2,1,0:T(8,128)(2,1)} %gather_fusion.1) | copy-start | bytes 9437188
Sparse Core Ops, SparseCore 0:
  9.4 42.1 all-gather.12
  53.7 100.1 all-gather.10
  156.0 71.7 all-gather.6
  229.7 37.9 all-gather.8
where the time goes:
time: 366 us; the launch traced here: 364 us
  waiting for transfers between devices  126 us (34%)
  matrix products  76 us (21%)
  local copies, waits for them, and re-layouts  70.7 us (19%)
  blocking collectives  39.8 us (11%)
  other arithmetic  31.4 us (9%)
  between operations  13.2 us (4%)
  starting transfers between devices  7.43 us (2%)
    all_to_all x1, waiting for transfers between devices, on_device(): lax.all_to_all(out_store[0], 'dp', split_axis=2, concat_axis=0, tiled=True)  50.9 us
    all_gather x1, waiting for transfers between devices, on_device(): in_whole = lax.all_gather(masked, 'dp', axis=0, tiled=True)  46.3 us
    dot_general x1, matrix products, on_device(): jnp.einsum('qfd,qkd->qkf', precond, right_rows, preferred_element_type=jn...  45.8 us
    unnamed x8, local copies, waits for them, and re-layouts  43 us
    psum x1, blocking collectives, on_device(): totals = lax.psum(partial_value, ('layer', 'dp'))  39.8 us
    all_gather x1, waiting for transfers between devices, on_device(): turned_in = lax.all_gather(turned_part, 'dp', axis=1, tiled=True)  27.2 us
    dot_general x1, matrix products, on_device(): jnp.dot(lax.all_gather(out_grads[0], 'dp', axis=1, tiled=True), rows, pre...  26.3 us
    div x1, other arithmetic, on_device(): precond = (product / divisor[None]).astype(jnp.bfloat16)  18.8 us
  transfers between devices with their start and end apart: 5, of which 3 were waited for; matrix products, arithmetic and copies ran while one was open for 35% of the time, Pallas kernels for 0%

commit v1 on v0

--- a/solution.py
+++ b/solution.py
@@ -2,6 +2,7 @@
 import jax.numpy as jnp
 from jax import lax
 from jax.sharding import PartitionSpec as P
+from jax.lax import psum
 
 NQ = 4
 TQ = 32
@@ -45,7 +46,7 @@
     right_rows = jnp.take(in_whole, chosen, axis=0).reshape(NQ, WIN * R, full_width)
     mapped = jnp.einsum("qfd,qkd->qkf", precond, right_rows, preferred_element_type=jnp.float32)
     partial_value = jnp.sum(mapped * left_rows.astype(jnp.float32), axis=2)
-    totals = lax.psum(partial_value, ("layer", "dp"))
+    totals = psum(psum(partial_value, "dp"), "layer")
     return totals.reshape(NQ, WIN, R)
 
 

time: 366 us -> 356 us (0.973)
  blocking collectives: 39.8 us -> 29.3 us
    psum x1 -> x2, blocking collectives: 39.8 us -> 29.3 us  [on_device(): totals = psum(psum(partial_value, 'dp'), 'layer')]
  transfers between devices with their start and end apart: 5 -> 5, of which waited for: 3 -> 3; matrix products, arithmetic and copies ran while one was open for 35% -> 36% of each run, Pallas kernels for 0% -> 0%
where the time goes in v1:
time: 356 us; the launch traced here: 354 us
  waiting for transfers between devices  126 us (35%)
  matrix products  76 us (21%)
  local copies, waits for them, and re-layouts  70.6 us (20%)
  other arithmetic  31.3 us (9%)
  blocking collectives  29.3 us (8%)
  between operations  13.2 us (4%)
  starting transfers between devices  7.43 us (2%)
    all_to_all x1, waiting for transfers between devices, on_device(): lax.all_to_all(out_store[0], 'dp', split_axis=2, concat_axis=0, tiled=True)  50.9 us
    all_gather x1, waiting for transfers between devices, on_device(): in_whole = lax.all_gather(masked, 'dp', axis=0, tiled=True)  46.3 us
    dot_general x1, matrix products, on_device(): jnp.einsum('qfd,qkd->qkf', precond, right_rows, preferred_element_type=jn...  45.8 us
    unnamed x8, local copies, waits for them, and re-layouts  42.9 us
    psum x2, blocking collectives, on_device(): totals = psum(psum(partial_value, 'dp'), 'layer')  29.3 us
    all_gather x1, waiting for transfers between devices, on_device(): turned_in = lax.all_gather(turned_part, 'dp', axis=1, tiled=True)  27.2 us
    dot_general x1, matrix products, on_device(): jnp.dot(lax.all_gather(out_grads[0], 'dp', axis=1, tiled=True), rows, pre...  26.3 us
    div x1, other arithmetic, on_device(): precond = (product / divisor[None]).astype(jnp.bfloat16)  18.7 us
  transfers between devices with their start and end apart: 5, of which 3 were waited for; matrix products, arithmetic and copies ran while one was open for 36% of the time, Pallas kernels for 0%

profile of v1, /device:TPU:0, one launch (start us, length us, event | category | flops | bytes accessed | tf_op | source)
XLA Modules:
  0.0 353.8 jit_solution(13576207420941662481)
XLA Ops:
  6.5 0.0 all-gather.13.cloned.1.call-start
  6.5 0.7 all-gather.13.cloned.1.call-update
  7.3 0.0 all-gather.11.cloned.1.call-start
  7.3 0.7 all-gather.11.cloned.1.call-update
  8.0 0.0 all-gather.7.cloned.1.call-start
  8.1 0.7 compare_convert_fusion
  8.8 2.0 bitcast_multiply_fusion
  10.8 0.0 all-gather.7.cloned.1.call-update
  10.8 17.2 %copy.13 = bf16[1,2,32,16384]{2,1,3,0:T(2,128)(2,1)} copy(bf16[1,2,32,16384]{3,2,1,0:T(8,128)(2,1)} %param.14) | data formatting | bytes 4194304 | tf_op args[5]
  28.0 8.0 %bitcast_bitcast_fusion = bf16[16384,2,32]{2,1,0:T(2,128)(2,1)} fusion(bf16[1,2,32,16384]{2,1,3,0:T(2,128)(2,1)} %copy.13), kind=kLoop, calls=%fused_computation.25 | loop fusion | bytes 4194304
  36.0 0.0 copy-start.1
  36.0 11.2 %reshape.112 = bf16[8,2,65536]{2,1,0:T(2,128)(2,1)} reshape(bf16[16384,2,32]{2,1,0:T(2,128)(2,1)} %bitcast_bitcast_fusion) | data formatting | bytes 4194304
  47.2 7.3 %all-to-all-start = ((bf16[8,2,65536]{2,1,0:T(2,128)(2,1)}), bf16[8,2,65536]{2,1,0:T(2,128)(2,1)S(1)}, u32[]{:S(2)}, u32[]{:S(2)}) async-start(bf16[8,2,65536]{2,1,0:T(2,128)(2,1)} %reshape.112), calls=%async_computation | async-start | bytes 4194304 | tf_op jit(solution)/shard_map/all_to_all | solution.py:41
  54.5 0.0 all-gather.9.cloned.1.call-start
  54.6 0.0 copy-done.1
  54.6 0.1 reshape.90
  54.7 0.1 broadcast_in_dim.28
  54.8 0.1 broadcast_in_dim.29
  54.9 18.7 %add_bitcast_fusion = f32[2048,4096]{1,0:T(8,128)} fusion(bf16[1,2048,4096]{2,1,0:T(8,128)(2,1)} %param.13), kind=kLoop, calls=%fused_computation.6 | loop fusion | flops 16777216 | bytes 50331648 | tf_op jit(solution)/shard_map/div | solution.py:38
  73.6 0.0 all-gather.13.cloned.1.call-done
  73.6 3.9 %fusion.13 = bf16[128,512]{1,0:T(8,128)(2,1)} fusion(bf16[1,4096,512]{2,1,0:T(8,128)(2,1)} %param.12, bf16[1,128,4096]{2,1,0:T(8,128)(2,1)} %all-gather.13.cloned.1.call-done), kind=kOutput, calls=%fused_computation.15 | convolution fusion | flops 536936448 | bytes 5373952 | tf_op jit(solution)/shard_map/dot_general | solution.py:28
  77.5 0.0 all-gather.9.cloned.1.call-update
  77.5 50.9 %all-to-all-done = bf16[8,2,65536]{2,1,0:T(2,128)(2,1)S(1)} async-done(((bf16[8,2,65536]{2,1,0:T(2,128)(2,1)}), bf16[8,2,65536]{2,1,0:T(2,128)(2,1)S(1)}, u32[]{:S(2)}, u32[]{:S(2)}) %all-to-all-start) | async-done | bytes 2097184 | tf_op jit(solution)/shard_map/all_to_all | solution.py:41
  128.5 6.5 %reshape.113 = bf16[16384,2,32]{2,1,0:T(2,128)(2,1)} reshape(bf16[8,2,65536]{2,1,0:T(2,128)(2,1)S(1)} %all-to-all-done) | data formatting | bytes 4194304
  135.0 17.8 %copy.18 = bf16[2,32,8,2048]{3,1,0,2:T(8,128)(2,1)S(1)} copy(bf16[2,32,8,2048]{1,0,3,2:T(2,128)(2,1)} %bitcast.47) | data formatting | bytes 4194304 | tf_op jit(solution)/shard_map/all_to_all | solution.py:41
  152.8 2.5 gather_fusion.1
  155.2 0.0 all-gather.11.cloned.1.call-done
  155.2 26.3 %fusion.8 = bf16[128,2048]{1,0:T(8,128)(2,1)} fusion(bf16[1,16384,2048]{2,1,0:T(8,128)(2,1)} %param.11, bf16[1,128,16384]{2,1,0:T(8,128)(2,1)} %all-gather.11.cloned.1.call-done), kind=kOutput, calls=%fused_computation.14 | convolution fusion | flops 8590196736 | bytes 71827456 | tf_op jit(solution)/shard_map/dot_general | solution.py:22
  181.5 46.3 %all-gather.7.cloned.1.call-done = bf16[16,32,4096]{2,1,0:T(8,128)(2,1)} async-done(((bf16[2,32,4096]{2,1,0:T(8,128)(2,1)}), bf16[16,32,4096]{2,1,0:T(8,128)(2,1)}) %all-gather.7.cloned.1.call-update) | async-done | bytes 4194320 | tf_op jit(solution)/shard_map/all_gather | solution.py:45
  227.8 6.5 %gather_fusion = bf16[24,32,4096]{2,1,0:T(8,128)(2,1)} fusion(bf16[16,32,4096]{2,1,0:T(8,128)(2,1)} %all-gather.7.cloned.1.call-done, s32[1024]{0:T(1024)S(1)} %pad_clamp_fusion), kind=kCustom, calls=%fused_computation | custom fusion | bytes 12583008 | tf_op jit(solution)/shard_map/jit(_take)/gather | solution.py:46
  234.3 6.1 %bitcast_select_fusion = bf16[4,192,4096]{2,1,0:T(8,128)(2,1)} fusion(pred[4,192]{1,0:T(4,128)(4,1)S(1)} %broadcast_in_dim.29, bf16[4,192,4096]{2,1,0:T(8,128)(2,1)} %bitcast.48), kind=kLoop, calls=%fused_computation.8 | loop fusion | flops 3145728 | bytes 12583680 | tf_op jit(solution)/shard_map/jit(_take)/select_n | solution.py:46
  240.4 27.2 %all-gather.9.cloned.1.call-done = bf16[128,4096]{1,0:T(8,128)(2,1)} async-done(((bf16[128,512]{1,0:T(8,128)(2,1)}), bf16[128,4096]{1,0:T(8,128)(2,1)}) %all-gather.9.cloned.1.call-update) | async-done | bytes 1048592 | tf_op jit(solution)/shard_map/all_gather | solution.py:33
  267.6 0.0 copy-start
  267.7 45.8 %fusion.2 = f32[4,192,2048]{2,1,0:T(8,128)} fusion(bf16[4,192,4096]{2,1,0:T(8,128)(2,1)} %bitcast_select_fusion, f32[2048,4096]{1,0:T(8,128)} %add_bitcast_fusion, bf16[4,32,2048]{2,1,0:T(8,128)(2,1)} %bitcast.51, bf16[4,32,4096]{2,1,0:T(8,128)(2,1)} %bitcast.52), kind=kOutput, calls=%fused_computation.5 | convolution fusion | flops 15099494400 | bytes 47710208 | tf_op jit(solution)/shard_map/qfd,qkd->qkf/dot_general | solution.py:47
  313.5 0.0 copy-done
  313.5 3.8 %multiply_reduce_fusion = f32[4,192]{1,0:T(4,128)S(1)} fusion(f32[4,192,2048]{2,1,0:T(8,128)} %fusion.2, pred[4,192]{1,0:T(4,128)(4,1)S(1)} %broadcast_in_dim.29, bf16[4,192,2048]{2,1,0:T(8,128)(2,1)S(1)} %bitcast.50), kind=kLoop, calls=%fused_computation.9 | loop fusion | flops 6290688 | bytes 9441024 | tf_op jit(solution)/shard_map/reduce_sum | solution.py:48
  317.2 19.2 %psum.14 = f32[4,192]{1,0:T(4,128)S(1)} all-reduce(f32[4,192]{1,0:T(4,128)S(1)} %multiply_reduce_fusion), channel_id=1, replica_groups=mesh['layer'=4,'dp'=8] {'dp'}, use_global_device_ids=true, to_apply=%region_1.2 | all-reduce | flops 768 | bytes 6144 | tf_op jit(solution)/shard_map/psum | solution.py:49
  336.5 0.1 reshape.93
  336.5 10.1 %psum.15 = f32[4,6,32]{2,1,0:T(8,128)S(1)} all-reduce(f32[4,6,32]{2,1,0:T(8,128)S(1)} %reshape.93), channel_id=1, replica_groups=mesh['layer'=4,'dp'=8] {'layer'}, use_global_device_ids=true, to_apply=%region_2.3 | all-reduce | flops 768 | bytes 6144 | tf_op jit(solution)/shard_map/psum | solution.py:49
  346.6 0.6 copy.16
  (4 shorter events, 0.0 us)
Async XLA Ops:
  6.5 67.1 %all-gather.13.cloned.1.call-start = ((), (), s32[]{:S(2)}) async-start(), calls=%async_computation.4 | async-start | bytes 1179648 | tf_op jit(solution)/shard_map/all_gather | solution.py:29
  7.3 148.0 %all-gather.11.cloned.1.call-start = ((), (), s32[]{:S(2)}) async-start(), calls=%async_computation.3 | async-start | bytes 4718592 | tf_op jit(solution)/shard_map/all_gather | solution.py:23
  8.0 219.8 %all-gather.7.cloned.1.call-start = ((), (), s32[]{:S(2)}) async-start(), calls=%async_computation.1 | async-start | bytes 4718592 | tf_op jit(solution)/shard_map/all_gather | solution.py:45
  36.0 18.6 %copy-start.1 = (s32[4,6]{1,0:T(4,128)S(1)}, s32[4,6]{1,0:T(4,128)}, u32[]{:S(2)}) copy-start(s32[4,6]{1,0:T(4,128)} %param.17) | copy-start | bytes 292
  47.2 81.2 %all-to-all-start = ((bf16[8,2,65536]{2,1,0:T(2,128)(2,1)}), bf16[8,2,65536]{2,1,0:T(2,128)(2,1)S(1)}, u32[]{:S(2)}, u32[]{:S(2)}) async-start(bf16[8,2,65536]{2,1,0:T(2,128)(2,1)} %reshape.112), calls=%async_computation | async-start | bytes 4194304 | tf_op jit(solution)/shard_map/all_to_all | solution.py:41
  54.5 213.1 %all-gather.9.cloned.1.call-start = ((), (), s32[]{:S(2)}) async-start(), calls=%async_computation.2 | async-start | bytes 1179648 | tf_op jit(solution)/shard_map/all_gather | solution.py:33
  267.6 45.8 %copy-start = (bf16[24,32,2048]{2,1,0:T(8,128)(2,1)S(1)}, bf16[24,32,2048]{2,1,0:T(8,128)(2,1)}, u32[]{:S(2)}) copy-start(bf16[24,32,2048]{2,1,0:T(8,128)(2,1)} %gather_fusion.1) | copy-start | bytes 9437188
Sparse Core Ops, SparseCore 0:
  9.4 42.1 all-gather.12
  53.7 100.0 all-gather.10
  156.0 71.7 all-gather.6
  229.7 37.9 all-gather.8
